TPU v7x, 128 devices: a whole 4x4x4 slice. The times are simulated.
128 devices in a mesh: row: 8 (over x, core), mp: 16 (over y, z).
Axes of the slice: x: 4, y: 4, z: 4, core: 2. Of those that a mesh axis runs over, the one named last changes fastest.
Arguments:
- queries: bfloat16 [2560, 16384], P('row', 'mp'), may hold values from -16 to 16
- new_kv: bfloat16 [2560, 2048], P('row', 'mp'), may hold values from -9 to 9
- cache_keys: bfloat16 [512, 16, 512, 128], P('row', 'mp'), may hold values from -26 to 26
- cache_values: bfloat16 [512, 16, 512, 128], P('row', 'mp'), may hold values from -12 to 12
- cache_lens: int32 [512], P('row'), may hold values from 8 to 1019, as said below
- accepted: int32 [512], P('row'), may hold values from 0 to 5
- dest: int32 [512], P('row'), may hold values from 0 to 511, as said below
- out_weight: bfloat16 [16384, 16384], P('mp', 'row'), may hold values from -0.046875 to 0.046875
Outputs:
- mixed: bfloat16 [2560, 16384], P('mp', 'row')
- next_kv: bfloat16 [512, 5, 2048], P('row', None, 'mp')
Inputs may be any that keep to these rules, and one draw needn't show every extreme that they name: `cache_lens`: every beam's cache leaves room for its 5 new tokens. dest is a permutation of 0 to 511; of the beams in each aligned block of 64 beams, exactly 8 go to slots of each aligned block of 64 slots.
All inputs are finite; a program needn't handle non-finite values.
Results may differ from a plain program's by a relative error of at most 0.02.
Values may be sent and summed in bfloat16 or wider, within the bound.
A program may use at most 128 MiB of HBM per device.

v0:
```python
import jax
import jax.numpy as jnp
from jax import lax
from jax.sharding import PartitionSpec as P

masked_score = -1e30


def partner(block, axis, bit):
    count = lax.axis_size(axis)
    route = []
    for low in range(count):
        high = low | 1 << bit
        if high != low and high < count:
            route += [(low, high), (high, low)]
    return lax.ppermute(block, axis, route)


def head_slice(values, start, count):
    return lax.dynamic_slice_in_dim(values, start, count, 3)


def shards(queries, new_kv, cache_keys, cache_values, cache_lens, accepted, dest, out_weight):
    beams_here = cache_keys.shape[0]
    halves_held = cache_keys.shape[1]
    half_length = cache_keys.shape[2]
    head_size = cache_keys.shape[3]
    drafts = queries.shape[0] // beams_here
    heads_owned = queries.shape[1] // head_size
    kv_columns = new_kv.shape[1]
    mp_place = lax.axis_index("mp")
    lower_side = mp_place % 2 == 0
    partner_queries, partner_fresh = partner((queries, new_kv), "mp", 0)
    group_queries = jnp.where(
        lower_side,
        jnp.concatenate([queries, partner_queries], 1),
        jnp.concatenate([partner_queries, queries], 1),
    )
    fresh_pair = jnp.where(
        lower_side,
        jnp.concatenate([new_kv, partner_fresh], 1),
        jnp.concatenate([partner_fresh, new_kv], 1),
    )
    group_heads = group_queries.shape[1] // head_size
    sides = (mp_place * halves_held + jnp.arange(halves_held, dtype=jnp.int32)) % 2
    query_block = group_queries.reshape(beams_here, drafts, group_heads, head_size)
    fresh_block = fresh_pair.reshape(beams_here, drafts, 2, head_size)
    fresh_keys = fresh_block[:, :, 0]
    fresh_values = fresh_block[:, :, 1]
    scale = head_size ** (-0.5)
    cache_scores = (
        jnp.einsum("btjd,bsid->bstji", query_block, cache_keys, preferred_element_type=jnp.float32)
        * scale
    )
    fresh_scores = (
        jnp.einsum("btjd,bud->btju", query_block, fresh_keys, preferred_element_type=jnp.float32)
        * scale
    )
    spots = sides[:, None] * half_length + jnp.arange(half_length, dtype=jnp.int32)[None, :]
    cache_valid = (spots[None] < cache_lens[:, None, None])[:, :, None, None, :]
    order = jnp.arange(drafts, dtype=jnp.int32)
    fresh_side = (cache_lens[:, None] + order[None, :]) // half_length
    causal = order[:, None] >= order[None, :]
    fresh_valid = (
        causal[None, None] & (fresh_side[:, None, None, :] == sides[None, :, None, None])
    )[:, :, :, None, :]
    cache_masked = jnp.where(cache_valid, cache_scores, masked_score)
    fresh_masked = jnp.where(fresh_valid, fresh_scores[:, None], masked_score)
    highest = jnp.maximum(jnp.max(cache_masked, -1), jnp.max(fresh_masked, -1))
    cache_weights = jnp.where(cache_valid, jnp.exp(cache_masked - highest[..., None]), 0.0).astype(
        jnp.bfloat16
    )
    fresh_weights = jnp.where(fresh_valid, jnp.exp(fresh_masked - highest[..., None]), 0.0).astype(
        jnp.bfloat16
    )
    partial_value = jnp.einsum(
        "bstji,bsid->bstjd", cache_weights, cache_values, preferred_element_type=jnp.float32
    )
    partial_value = partial_value + jnp.einsum(
        "bstju,bud->bstjd", fresh_weights, fresh_values, preferred_element_type=jnp.float32
    )
    weight_mass = jnp.sum(cache_weights.astype(jnp.float32), -1) + jnp.sum(
        fresh_weights.astype(jnp.float32), -1
    )
    own_start = jnp.where(lower_side, 0, heads_owned).astype(jnp.int32)
    other_start = heads_owned - own_start
    got_partial, got_highest, got_mass = partner(
        (
            head_slice(partial_value, other_start, heads_owned),
            head_slice(highest, other_start, heads_owned),
            head_slice(weight_mass, other_start, heads_owned),
        ),
        "mp",
        0,
    )
    own_partial = head_slice(partial_value, own_start, heads_owned)
    own_highest = head_slice(highest, own_start, heads_owned)
    own_mass = head_slice(weight_mass, own_start, heads_owned)
    partial_value = jnp.where(
        lower_side,
        jnp.concatenate([own_partial, got_partial], 1),
        jnp.concatenate([got_partial, own_partial], 1),
    )
    highest = jnp.where(
        lower_side,
        jnp.concatenate([own_highest, got_highest], 1),
        jnp.concatenate([got_highest, own_highest], 1),
    )
    weight_mass = jnp.where(
        lower_side,
        jnp.concatenate([own_mass, got_mass], 1),
        jnp.concatenate([got_mass, own_mass], 1),
    )
    summit = jnp.max(highest, 1)
    factor = jnp.exp(highest - summit[:, None])
    numer = jnp.sum(factor[..., None] * partial_value, 1)
    denom = jnp.sum(factor * weight_mass, 1)
    attention = (
        (numer / denom[..., None])
        .astype(jnp.bfloat16)
        .reshape(beams_here * drafts, heads_owned * head_size)
    )
    projected = jnp.dot(
        lax.all_gather(attention, "row", axis=0, tiled=True),
        out_weight,
        preferred_element_type=jnp.float32,
    )
    rows_owned = projected.shape[0] // lax.axis_size("mp")
    totals = lax.psum(projected.astype(jnp.bfloat16), "mp").astype(jnp.float32)
    owned_rows = lax.dynamic_slice_in_dim(totals, mp_place * rows_owned, rows_owned, 0)
    mixed = owned_rows.astype(jnp.bfloat16)
    fresh_rows = new_kv.reshape(beams_here, drafts, kv_columns)
    kept_mask = order[None, :] < accepted[:, None]
    kept_rows = jnp.where(kept_mask[..., None], fresh_rows, jnp.zeros_like(fresh_rows)).reshape(
        beams_here, drafts * kv_columns
    )
    blocks = lax.axis_size("row")
    share_count = beams_here // blocks
    target = dest // beams_here
    landing = dest % beams_here
    beam_index = jnp.arange(beams_here, dtype=jnp.int32)
    earlier = (target[None, :] == target[:, None]) & (beam_index[None, :] < beam_index[:, None])
    position = jnp.sum(earlier.astype(jnp.int32), 1)
    send_slot = target * share_count + position
    picker = send_slot[None, :] == beam_index[:, None]
    outgoing = jnp.dot(
        picker.astype(jnp.bfloat16), kept_rows, preferred_element_type=jnp.float32
    ).astype(jnp.bfloat16)
    outgoing = outgoing.reshape(blocks, share_count, drafts * kv_columns)
    labels = jnp.sum(jnp.where(picker, landing[None, :], 0), 1).reshape(blocks, share_count)
    arrived, arrived_labels = (
        lax.all_to_all(outgoing, "row", split_axis=0, concat_axis=0, tiled=True),
        lax.all_to_all(labels, "row", split_axis=0, concat_axis=0, tiled=True),
    )
    arrived = arrived.reshape(beams_here, drafts * kv_columns)
    arrived_labels = arrived_labels.reshape(beams_here)
    placer = (arrived_labels[None, :] == beam_index[:, None]).astype(jnp.bfloat16)
    next_kv = jnp.dot(placer, arrived, preferred_element_type=jnp.float32).astype(jnp.bfloat16)
    next_kv = next_kv.reshape(beams_here, drafts, kv_columns)
    return (mixed, next_kv)


def solution(mesh):
    placed = (
        P("row", "mp"),
        P("row", "mp"),
        P("row", "mp", None, None),
        P("row", "mp", None, None),
        P("row"),
        P("row"),
        P("row"),
        P("mp", "row"),
    )
    return jax.shard_map(
        shards,
        mesh=mesh,
        in_specs=placed,
        out_specs=(P("mp", "row"), P("row", None, "mp")),
        check_vma=False,
    )
```

profile of v0, /device:TPU:1, one launch (start us, length us, event | category | flops | bytes accessed | tf_op | source)
XLA Modules:
  0.0 307.1 jit_solution(3005448129393214941)
XLA Ops:
  7.2 0.0 all-gather.2.cloned.1.call-start
  7.2 2.5 collective-permute-start
  9.8 0.1 collective-permute-start.1
  9.9 0.7 fusion.18
  10.7 0.7 broadcast_compare_fusion
  11.4 14.7 %collective-permute-done.1 = bf16[320,128]{1,0:T(8,128)(2,1)S(1)} collective-permute-done((bf16[320,128]{1,0:T(8,128)(2,1)}, bf16[320,128]{1,0:T(8,128)(2,1)S(1)}, u32[]{:S(2)}, u32[]{:S(2)}) %collective-permute-start.1) | collective-permute-done | bytes 81952 | tf_op jit(solution)/shard_map/ppermute | solution.py:16
  26.2 1.0 maximum_select_fusion.2
  27.2 0.2 fusion.26
  27.5 0.0 collective-permute-done
  27.5 1.8 fusion.10
  29.3 0.3 copy.56
  29.6 6.5 %fusion.1 = (f32[64,5,16]{2,1,0:T(8,128)S(1)}, f32[64,5,16,512]{3,2,1,0:T(8,128)S(1)}) fusion(pred[64,512]{1,0:T(8,128)(4,1)S(1)} %broadcast_compare_fusion, bf16[64,5,16,128]{3,2,1,0:T(8,128)(2,1)S(1)} %bitcast.96, bf16[64,1,512,128]{3,2,1,0:T(8,128)(2,1)} %param.10), kind=kOutput, calls=%fused_computation.5 | convolution fusion | flops 678947840 | bytes 20238336 | tf_op jit(solution)/shard_map/btjd,bsid->bstji/dot_general | solution.py:52
  36.1 0.0 copy-start
  36.1 3.2 %fusion.27 = (f32[64,5,16]{2,1,0:T(8,128)S(1)}, f32[64,5,16,5]{2,3,1,0:T(8,128)S(1)}) fusion(bf16[64,5,16,128]{3,2,1,0:T(8,128)(2,1)S(1)} %bitcast.97, bf16[64,5,1,128]{3,2,1,0:T(2,128)(2,1)S(1)} %get-tuple-element.23, pred[64,5,5]{2,1,0:T(8,128)(4,1)S(1)} %broadcast_and_fusion), kind=kOutput, calls=%fused_computation.78 | convolution fusion | flops 6625280 | bytes 1517120 | tf_op jit(solution)/shard_map/btjd,bud->btju/dot_general | solution.py:56
  39.3 1.5 convert_reduce_fusion.1
  40.8 5.6 %fusion.2 = f32[64,5,16,128]{3,2,1,0:T(8,128)S(1)} fusion(bf16[64,1,512,128]{3,2,1,0:T(8,128)(2,1)} %param.11, f32[64,5,16,512]{3,2,1,0:T(8,128)S(1)} %get-tuple-element.27, f32[64,5,16]{2,1,0:T(8,128)S(1)} %max.16, pred[64,512]{1,0:T(8,128)(4,1)S(1)} %broadcast_compare_fusion), kind=kOutput, calls=%fused_computation.6 | convolution fusion | flops 684195840 | bytes 21549056 | tf_op jit(solution)/shard_map/bstji,bsid->bstjd/dot_general | solution.py:76
  46.4 0.0 copy-done
  46.4 1.7 convolution_add_fusion
  48.1 1.3 dynamic-slice_bitcast_fusion.1
  49.4 1.2 collective-permute-start.3
  50.5 0.2 constant_dynamic-slice_fusion.2
  50.7 0.1 copy.41
  50.9 0.3 collective-permute-start.2
  51.2 6.7 %convert_reduce_fusion = f32[64,5,16]{2,1,0:T(8,128)S(1)} fusion(f32[64,5,16]{2,1,0:T(8,128)S(1)} %max.16, f32[64,5,16,512]{3,2,1,0:T(8,128)} %copy-done, pred[64,512]{1,0:T(8,128)(4,1)S(1)} %broadcast_compare_fusion), kind=kLoop, calls=%fused_computation.3 | loop fusion | flops 18344960 | bytes 10559488 | tf_op jit(solution)/shard_map/reduce_sum | solution.py:82
  57.9 0.0 copy-done.1
  57.9 0.2 constant_dynamic-slice_fusion.1
  58.1 0.1 copy.45
  58.3 1.2 collective-permute-start.4
  59.5 0.1 copy.40
  59.6 0.1 copy.44
  59.7 19.4 %collective-permute-done.2 = f32[64,1,5,8]{0,3,2,1:T(8,128)S(1)} collective-permute-done((f32[64,1,5,8]{0,3,2,1:T(8,128)S(1)}, f32[64,1,5,8]{0,3,2,1:T(8,128)S(1)}, u32[]{:S(2)}, u32[]{:S(2)}) %collective-permute-start.2) | collective-permute-done | bytes 10272 | tf_op jit(solution)/shard_map/ppermute | solution.py:16
  79.1 0.4 collective-permute-done.4
  79.5 0.2 copy.42
  79.7 0.1 copy.46
  79.9 0.0 collective-permute-done.3
  79.9 1.0 fusion.8
  81.0 0.4 divide_convert_fusion
  81.4 1.0 copy.69
  82.3 0.0 all-gather.2.cloned.1.call-update
  82.4 0.2 all-reduce.2.cloned.1.call-start
  82.6 40.2 %all-gather.2.cloned.1.call-done = bf16[2560,1024]{1,0:T(8,128)(2,1)} async-done(((bf16[320,1024]{1,0:T(8,128)(2,1)}), bf16[2560,1024]{1,0:T(8,128)(2,1)}) %all-gather.2.cloned.1.call-update) | async-done | bytes 5242896 | tf_op jit(solution)/shard_map/all_gather | solution.py:124
  122.8 16.6 %convolution_convert_fusion = bf16[2560,2048]{1,0:T(8,128)(2,1)} fusion(bf16[2560,1024]{1,0:T(8,128)(2,1)} %all-gather.2.cloned.1.call-done, bf16[1024,2048]{1,0:T(8,128)(2,1)} %param.15), kind=kOutput, calls=%fused_computation | convolution fusion | flops 10742661120 | bytes 19922944 | tf_op jit(solution)/shard_map/dot_general | solution.py:123
  139.4 0.0 all-reduce.2.cloned.1.call-update
  139.4 0.6 copy-done.4
  140.0 0.2 convert_reduce_fusion.2
  140.2 0.1 select_reduce_fusion
  140.3 0.7 all_to_all.9
  141.0 3.5 %all-to-all-start = ((s32[8,1,8]{2,1,0:T(1,128)}), s32[8,1,8]{2,1,0:T(1,128)S(1)}, u32[]{:S(2)}, u32[]{:S(2)}) async-start(s32[8,1,8]{2,1,0:T(1,128)} %bitcast.25), calls=%async_computation | async-start | bytes 8192 | tf_op jit(solution)/shard_map/all_to_all | solution.py:153
  144.5 0.0 copy-done.2
  144.5 0.1 reshape.269
  144.6 0.0 copy-done.3
  144.6 0.1 iota_compare_fusion
  144.7 0.1 broadcast_in_dim.102
  144.8 0.8 fusion.11
  145.6 3.4 %all-to-all-done = s32[8,1,8]{2,1,0:T(1,128)S(1)} async-done(((s32[8,1,8]{2,1,0:T(1,128)}), s32[8,1,8]{2,1,0:T(1,128)S(1)}, u32[]{:S(2)}, u32[]{:S(2)}) %all-to-all-start) | async-done | bytes 288 | tf_op jit(solution)/shard_map/all_to_all | solution.py:153
  149.0 4.0 %all-to-all-start.1 = ((bf16[8,8,640]{2,1,0:T(8,128)(2,1)}), bf16[8,8,640]{2,1,0:T(8,128)(2,1)S(1)}, u32[]{:S(2)}, u32[]{:S(2)}) async-start(bf16[8,8,640]{2,1,0:T(8,128)(2,1)} %fusion.11), calls=%async_computation.1 | async-start | bytes 163840 | tf_op jit(solution)/shard_map/all_to_all | solution.py:152
  153.0 0.5 broadcast.179
  153.5 0.7 reduce.9
  154.1 0.1 eq.70
  154.2 3.7 %all-to-all-done.1 = bf16[8,8,640]{2,1,0:T(8,128)(2,1)S(1)} async-done(((bf16[8,8,640]{2,1,0:T(8,128)(2,1)}), bf16[8,8,640]{2,1,0:T(8,128)(2,1)S(1)}, u32[]{:S(2)}, u32[]{:S(2)}) %all-to-all-start.1) | async-done | bytes 81952 | tf_op jit(solution)/shard_map/all_to_all | solution.py:152
  157.9 0.1 fusion.12
  158.1 0.7 copy.70
  158.7 139.5 %all-reduce.2.cloned.1.call-done = bf16[2560,2048]{1,0:T(8,128)(2,1)} async-done(((bf16[2560,2048]{1,0:T(8,128)(2,1)}), bf16[2560,2048]{1,0:T(8,128)(2,1)}) %all-reduce.2.cloned.1.call-update) | async-done | bytes 10485776 | tf_op jit(solution)/shard_map/psum | solution.py:129
  298.3 2.0 convert_convert_fusion
  (14 shorter events, 0.2 us)
Async XLA Ops:
  7.2 115.6 %all-gather.2.cloned.1.call-start = ((), (), s32[]{:S(2)}) async-start(), calls=%async_computation.2 | async-start | bytes 5898240 | tf_op jit(solution)/shard_map/all_gather | solution.py:124
  7.2 20.3 %collective-permute-start = (bf16[320,1024]{1,0:T(8,128)(2,1)}, bf16[320,1024]{1,0:T(8,128)(2,1)S(1)}, u32[]{:S(2)}, u32[]{:S(2)}) collective-permute-start(bf16[320,1024]{1,0:T(8,128)(2,1)} %param.8), channel_id=1, source_target_pairs={{0,1},{1,0},{2,3},{3,2},{4,5},{5,4},{6,7},{7,6},{8,9},{9,8},{10,11... | collective-permute-start | bytes 1966088 | tf_op jit(solution)/shard_map/ppermute | solution.py:16
  9.8 16.4 %collective-permute-start.1 = (bf16[320,128]{1,0:T(8,128)(2,1)}, bf16[320,128]{1,0:T(8,128)(2,1)S(1)}, u32[]{:S(2)}, u32[]{:S(2)}) collective-permute-start(bf16[320,128]{1,0:T(8,128)(2,1)} %param.9), channel_id=1, source_target_pairs={{0,1},{1,0},{2,3},{3,2},{4,5},{5,4},{6,7},{7,6},{8,9},{9,8},{10,11... | collective-permute-start | bytes 245768 | tf_op jit(solution)/shard_map/ppermute | solution.py:16
  36.1 10.3 %copy-start = (f32[64,5,16,512]{3,2,1,0:T(8,128)}, f32[64,5,16,512]{3,2,1,0:T(8,128)S(1)}, u32[]{:S(2)}) copy-start(f32[64,5,16,512]{3,2,1,0:T(8,128)S(1)} %get-tuple-element.27) | copy-start | bytes 31457284
  49.4 30.5 %collective-permute-start.3 = (f32[64,1,5,8,128]{4,3,2,0,1:T(8,128)}, f32[64,1,5,8,128]{4,3,2,0,1:T(8,128)S(1)}, u32[]{:S(2)}, u32[]{:S(2)}) collective-permute-start(f32[64,1,5,8,128]{4,3,2,0,1:T(8,128)} %get-tuple-element.17), channel_id=1, source_target_pairs={{0,1},{1,0},{2,3},{3,2},{4,5},{5,4},{6,7},{7,6},{8,9},{9,8},{10,11... | collective-permute-start | bytes 3932168 | tf_op jit(solution)/shard_map/ppermute | solution.py:16
  50.9 7.0 %copy-start.1 = (f32[64,5,16]{2,1,0:T(8,128)S(1)}, f32[64,5,16]{2,1,0:T(8,128)}, u32[]{:S(2)}) copy-start(f32[64,5,16]{2,1,0:T(8,128)} %convert_reduce_fusion.1) | copy-start | bytes 61444
  50.9 28.2 %collective-permute-start.2 = (f32[64,1,5,8]{0,3,2,1:T(8,128)S(1)}, f32[64,1,5,8]{0,3,2,1:T(8,128)S(1)}, u32[]{:S(2)}, u32[]{:S(2)}) collective-permute-start(f32[64,1,5,8]{0,3,2,1:T(8,128)S(1)} %bitcast.105), channel_id=1, source_target_pairs={{0,1},{1,0},{2,3},{3,2},{4,5},{5,4},{6,7},{7,6},{8,9},{9,8},{10,11... | collective-permute-start | bytes 30728 | tf_op jit(solution)/shard_map/ppermute | solution.py:16
  58.3 21.2 %collective-permute-start.4 = (f32[64,1,5,8]{0,3,2,1:T(8,128)S(1)}, f32[64,1,5,8]{0,3,2,1:T(8,128)S(1)}, u32[]{:S(2)}, u32[]{:S(2)}) collective-permute-start(f32[64,1,5,8]{0,3,2,1:T(8,128)S(1)} %bitcast.106), channel_id=1, source_target_pairs={{0,1},{1,0},{2,3},{3,2},{4,5},{5,4},{6,7},{7,6},{8,9},{9,8},{10,11... | collective-permute-start | bytes 30728 | tf_op jit(solution)/shard_map/ppermute | solution.py:16
  82.4 215.9 %all-reduce.2.cloned.1.call-start = ((), (), s32[]{:S(2)}) async-start(), calls=%async_computation.3 | async-start | bytes 20971520 | tf_op jit(solution)/shard_map/psum | solution.py:129
  139.4 0.7 copy-start.4
  139.4 5.1 %copy-start.2 = (bf16[320,128]{1,0:T(8,128)(2,1)S(1)}, bf16[320,128]{1,0:T(8,128)(2,1)}, u32[]{:S(2)}) copy-start(bf16[320,128]{1,0:T(8,128)(2,1)} %param.9) | copy-start | bytes 245764
  139.4 5.2 %copy-start.3 = (s32[64]{0:T(128)S(1)}, s32[64]{0:T(128)}, u32[]{:S(2)}) copy-start(s32[64]{0:T(128)} %param.13) | copy-start | bytes 772
  141.0 8.0 %all-to-all-start = ((s32[8,1,8]{2,1,0:T(1,128)}), s32[8,1,8]{2,1,0:T(1,128)S(1)}, u32[]{:S(2)}, u32[]{:S(2)}) async-start(s32[8,1,8]{2,1,0:T(1,128)} %bitcast.25), calls=%async_computation | async-start | bytes 8192 | tf_op jit(solution)/shard_map/all_to_all | solution.py:153
  149.0 8.9 %all-to-all-start.1 = ((bf16[8,8,640]{2,1,0:T(8,128)(2,1)}), bf16[8,8,640]{2,1,0:T(8,128)(2,1)S(1)}, u32[]{:S(2)}, u32[]{:S(2)}) async-start(bf16[8,8,640]{2,1,0:T(8,128)(2,1)} %fusion.11), calls=%async_computation.1 | async-start | bytes 163840 | tf_op jit(solution)/shard_map/all_to_all | solution.py:152
Sparse Core Ops, SparseCore 0:
  82.5 40.2 all-gather.1
  139.5 158.7 all-reduce.1
where the time goes:
time: 308 us; the launch traced here: 307 us
  waiting for transfers between devices  221 us (72%)
  matrix products  34.4 us (11%)
  other arithmetic  17.1 us (6%)
  between operations  14.3 us (5%)
  starting transfers between devices  13 us (4%)
  local copies, waits for them, and re-layouts  6.79 us (2%)
    psum x1, waiting for transfers between devices, shards(): totals = lax.psum(projected.astype(jnp.bfloat16), 'mp').astype(jnp.float32)  140 us
    all_gather x1, waiting for transfers between devices, shards(): lax.all_gather(attention, 'row', axis=0, tiled=True)  40.2 us
    ppermute x5, waiting for transfers between devices, partner(): return lax.ppermute(block, axis, route)  34.5 us
    dot_general x1, matrix products, shards(): jnp.dot(lax.all_gather(attention, 'row', axis=0, tiled=True), out_weight,...  16.6 us
    reduce_sum x1, other arithmetic, shards(): jnp.sum(cache_weights.astype(jnp.float32), -1)  6.68 us
    dot_general x1, matrix products, shards(): jnp.einsum('btjd,bsid->bstji', query_block, cache_keys, preferred_element...  6.47 us
  transfers between devices with their start and end apart: 9, of which 7 were waited for; matrix products, arithmetic and copies ran while one was open for 5% of the time, Pallas kernels for 0%

commit v1 on v0

--- a/solution.py
+++ b/solution.py
@@ -121,7 +121,9 @@
         .reshape(beams_here * drafts, heads_owned * head_size)
     )
     projected = jnp.dot(
-        lax.all_gather(attention, "row", axis=0, tiled=True),
+        jnp.concatenate(
+            lax.all_to_all(jnp.stack([attention] * lax.axis_size("row")), "row", 0, 0), axis=0
+        ),
         out_weight,
         preferred_element_type=jnp.float32,
     )

time: 308 us -> 332 us (1.078)
  blocking collectives: 0 us -> 67.2 us
  waiting for transfers between devices: 221 us -> 181 us
    all_to_all x0 -> x1, blocking collectives: none -> 67.2 us  [shards(): lax.all_to_all(jnp.stack([attention] * lax.axis_size('row')), 'row', 0, 0)]
    all_gather x1 -> x0, waiting for transfers between devices: 40.2 us -> none  [shards(): lax.all_gather(attention, 'row', axis=0, tiled=True)]
    dot_general x1, matrix products: 16.6 us -> 13.2 us  [shards(): jnp.dot(jnp.concatenate(lax.all_to_all(jnp.stack([attention] * lax.axis_s...]
  transfers between devices with their start and end apart: 9 -> 8, of which waited for: 7 -> 6; matrix products, arithmetic and copies ran while one was open for 5% -> 4% of each run, Pallas kernels for 0% -> 0%
where the time goes in v1:
time: 332 us; the launch traced here: 331 us
  waiting for transfers between devices  181 us (55%)
  blocking collectives  67.2 us (20%)
  matrix products  31.1 us (9%)
  other arithmetic  17.1 us (5%)
  between operations  14.3 us (4%)
  starting transfers between devices  13.6 us (4%)
  local copies, waits for them, and re-layouts  6.62 us (2%)
    psum x1, waiting for transfers between devices, shards(): totals = lax.psum(projected.astype(jnp.bfloat16), 'mp').astype(jnp.float32)  140 us
    all_to_all x1, blocking collectives, shards(): lax.all_to_all(jnp.stack([attention] * lax.axis_size('row')), 'row', 0, 0)  67.2 us
    ppermute x5, waiting for transfers between devices, partner(): return lax.ppermute(block, axis, route)  34.5 us
    dot_general x1, matrix products, shards(): jnp.dot(jnp.concatenate(lax.all_to_all(jnp.stack([attention] * lax.axis_s...  13.2 us
    reduce_sum x1, other arithmetic, shards(): jnp.sum(cache_weights.astype(jnp.float32), -1)  6.68 us
  transfers between devices with their start and end apart: 8, of which 6 were waited for; matrix products, arithmetic and copies ran while one was open for 4% of the time, Pallas kernels for 0%

profile of v1, /device:TPU:1, one launch (start us, length us, event | category | flops | bytes accessed | tf_op | source)
XLA Modules:
  0.0 331.1 jit_solution(8797938787377897587)
XLA Ops:
  7.2 0.0 all-reduce.2.cloned.1.call-start
  7.2 2.5 collective-permute-start
  9.8 0.1 collective-permute-start.1
  9.9 0.7 fusion.18
  10.7 0.7 broadcast_compare_fusion
  11.4 14.7 %collective-permute-done.1 = bf16[320,128]{1,0:T(8,128)(2,1)S(1)} collective-permute-done((bf16[320,128]{1,0:T(8,128)(2,1)}, bf16[320,128]{1,0:T(8,128)(2,1)S(1)}, u32[]{:S(2)}, u32[]{:S(2)}) %collective-permute-start.1) | collective-permute-done | bytes 81952 | tf_op jit(solution)/shard_map/ppermute | solution.py:16
  26.2 1.0 maximum_select_fusion.2
  27.2 0.2 fusion.26
  27.5 0.0 collective-permute-done
  27.5 1.8 fusion.10
  29.3 0.3 copy.56
  29.6 6.5 %fusion.1 = (f32[64,5,16]{2,1,0:T(8,128)S(1)}, f32[64,5,16,512]{3,2,1,0:T(8,128)S(1)}) fusion(pred[64,512]{1,0:T(8,128)(4,1)S(1)} %broadcast_compare_fusion, bf16[64,5,16,128]{3,2,1,0:T(8,128)(2,1)S(1)} %bitcast.97, bf16[64,1,512,128]{3,2,1,0:T(8,128)(2,1)} %param.10), kind=kOutput, calls=%fused_computation.5 | convolution fusion | flops 678947840 | bytes 20238336 | tf_op jit(solution)/shard_map/btjd,bsid->bstji/dot_general | solution.py:52
  36.1 0.0 copy-start
  36.1 3.2 fusion.27
  39.3 1.5 convert_reduce_fusion.1
  40.8 5.6 %fusion.2 = f32[64,5,16,128]{3,2,1,0:T(8,128)S(1)} fusion(bf16[64,1,512,128]{3,2,1,0:T(8,128)(2,1)} %param.11, f32[64,5,16,512]{3,2,1,0:T(8,128)S(1)} %get-tuple-element.27, f32[64,5,16]{2,1,0:T(8,128)S(1)} %max.16, pred[64,512]{1,0:T(8,128)(4,1)S(1)} %broadcast_compare_fusion), kind=kOutput, calls=%fused_computation.6 | convolution fusion | flops 684195840 | bytes 21549056 | tf_op jit(solution)/shard_map/bstji,bsid->bstjd/dot_general | solution.py:76
  46.4 0.0 copy-done
  46.4 1.7 convolution_add_fusion
  48.1 1.3 dynamic-slice_bitcast_fusion.1
  49.4 1.2 collective-permute-start.3
  50.5 0.2 constant_dynamic-slice_fusion.2
  50.7 0.1 copy.41
  50.9 0.3 collective-permute-start.2
  51.2 6.7 %convert_reduce_fusion = f32[64,5,16]{2,1,0:T(8,128)S(1)} fusion(f32[64,5,16]{2,1,0:T(8,128)S(1)} %max.16, f32[64,5,16,512]{3,2,1,0:T(8,128)} %copy-done, pred[64,512]{1,0:T(8,128)(4,1)S(1)} %broadcast_compare_fusion), kind=kLoop, calls=%fused_computation.3 | loop fusion | flops 18344960 | bytes 10559488 | tf_op jit(solution)/shard_map/reduce_sum | solution.py:82
  57.9 0.0 copy-done.1
  57.9 0.2 constant_dynamic-slice_fusion.1
  58.1 0.1 copy.45
  58.3 1.2 collective-permute-start.4
  59.5 0.1 copy.40
  59.6 0.1 copy.44
  59.7 19.4 %collective-permute-done.2 = f32[64,1,5,8]{0,3,2,1:T(8,128)S(1)} collective-permute-done((f32[64,1,5,8]{0,3,2,1:T(8,128)S(1)}, f32[64,1,5,8]{0,3,2,1:T(8,128)S(1)}, u32[]{:S(2)}, u32[]{:S(2)}) %collective-permute-start.2) | collective-permute-done | bytes 10272 | tf_op jit(solution)/shard_map/ppermute | solution.py:16
  79.1 0.4 collective-permute-done.4
  79.5 0.2 copy.42
  79.7 0.1 copy.46
  79.9 0.0 collective-permute-done.3
  79.9 1.0 fusion.8
  81.0 0.4 divide_convert_fusion
  81.4 0.1 copy.69
  81.5 0.7 stack.3
  82.2 0.0 copy-start.4
  82.2 67.2 %all_to_all.19 = bf16[8,320,1024]{2,1,0:T(8,128)(2,1)S(1)} all-to-all(bf16[8,320,1024]{2,1,0:T(8,128)(2,1)S(1)} %stack.3), channel_id=1, replica_groups=mesh['row'=8,'mp'=16] {'row'}, dimensions={0} | all-to-all | bytes 10485760 | tf_op jit(solution)/shard_map/all_to_all | solution.py:125
  149.3 13.2 %convolution_convert_fusion = bf16[2560,2048]{1,0:T(8,128)(2,1)} fusion(bf16[2560,1024]{1,0:T(8,128)(2,1)S(1)} %bitcast.99, bf16[1024,2048]{1,0:T(8,128)(2,1)S(1)} %copy-done.4), kind=kOutput, calls=%fused_computation | convolution fusion | flops 10742661120 | bytes 19922944 | tf_op jit(solution)/shard_map/dot_general | solution.py:123
  162.6 0.0 all-reduce.2.cloned.1.call-update
  162.6 0.6 copy-done.5
  163.2 0.2 convert_reduce_fusion.2
  163.4 0.1 select_reduce_fusion
  163.5 0.7 all_to_all.13
  164.2 4.3 %all-to-all-start.1 = ((s32[8,1,8]{2,1,0:T(1,128)}), s32[8,1,8]{2,1,0:T(1,128)S(1)}, u32[]{:S(2)}, u32[]{:S(2)}) async-start(s32[8,1,8]{2,1,0:T(1,128)} %bitcast.26), calls=%async_computation.1 | async-start | bytes 8192 | tf_op jit(solution)/shard_map/all_to_all | solution.py:155
  168.5 0.0 copy-done.2
  168.5 0.1 reshape.275
  168.5 0.0 copy-done.3
  168.5 0.1 iota_compare_fusion
  168.6 0.1 broadcast_in_dim.102
  168.8 0.8 fusion.11
  169.6 3.4 %all-to-all-done.1 = s32[8,1,8]{2,1,0:T(1,128)S(1)} async-done(((s32[8,1,8]{2,1,0:T(1,128)}), s32[8,1,8]{2,1,0:T(1,128)S(1)}, u32[]{:S(2)}, u32[]{:S(2)}) %all-to-all-start.1) | async-done | bytes 288 | tf_op jit(solution)/shard_map/all_to_all | solution.py:155
  173.0 4.0 %all-to-all-start.2 = ((bf16[8,8,640]{2,1,0:T(8,128)(2,1)}), bf16[8,8,640]{2,1,0:T(8,128)(2,1)S(1)}, u32[]{:S(2)}, u32[]{:S(2)}) async-start(bf16[8,8,640]{2,1,0:T(8,128)(2,1)} %fusion.11), calls=%async_computation.2 | async-start | bytes 163840 | tf_op jit(solution)/shard_map/all_to_all | solution.py:154
  176.9 0.5 broadcast.181
  177.4 0.7 reduce.9
  178.1 0.1 eq.70
  178.2 3.7 %all-to-all-done.2 = bf16[8,8,640]{2,1,0:T(8,128)(2,1)S(1)} async-done(((bf16[8,8,640]{2,1,0:T(8,128)(2,1)}), bf16[8,8,640]{2,1,0:T(8,128)(2,1)S(1)}, u32[]{:S(2)}, u32[]{:S(2)}) %all-to-all-start.2) | async-done | bytes 81952 | tf_op jit(solution)/shard_map/all_to_all | solution.py:154
  181.9 0.1 fusion.12
  182.1 0.7 copy.70
  182.7 139.6 %all-reduce.2.cloned.1.call-done = bf16[2560,2048]{1,0:T(8,128)(2,1)} async-done(((bf16[2560,2048]{1,0:T(8,128)(2,1)}), bf16[2560,2048]{1,0:T(8,128)(2,1)}) %all-reduce.2.cloned.1.call-update) | async-done | bytes 10485776 | tf_op jit(solution)/shard_map/psum | solution.py:131
  322.3 2.0 convert_convert_fusion
  (15 shorter events, 0.2 us)
Async XLA Ops:
  7.2 315.1 %all-reduce.2.cloned.1.call-start = ((), (), s32[]{:S(2)}) async-start(), calls=%async_computation.3 | async-start | bytes 20971520 | tf_op jit(solution)/shard_map/psum | solution.py:131
  7.2 20.3 %collective-permute-start = (bf16[320,1024]{1,0:T(8,128)(2,1)}, bf16[320,1024]{1,0:T(8,128)(2,1)S(1)}, u32[]{:S(2)}, u32[]{:S(2)}) collective-permute-start(bf16[320,1024]{1,0:T(8,128)(2,1)} %param.8), channel_id=1, source_target_pairs={{0,1},{1,0},{2,3},{3,2},{4,5},{5,4},{6,7},{7,6},{8,9},{9,8},{10,11... | collective-permute-start | bytes 1966088 | tf_op jit(solution)/shard_map/ppermute | solution.py:16
  9.8 16.4 %collective-permute-start.1 = (bf16[320,128]{1,0:T(8,128)(2,1)}, bf16[320,128]{1,0:T(8,128)(2,1)S(1)}, u32[]{:S(2)}, u32[]{:S(2)}) collective-permute-start(bf16[320,128]{1,0:T(8,128)(2,1)} %param.9), channel_id=1, source_target_pairs={{0,1},{1,0},{2,3},{3,2},{4,5},{5,4},{6,7},{7,6},{8,9},{9,8},{10,11... | collective-permute-start | bytes 245768 | tf_op jit(solution)/shard_map/ppermute | solution.py:16
  36.1 10.3 %copy-start = (f32[64,5,16,512]{3,2,1,0:T(8,128)}, f32[64,5,16,512]{3,2,1,0:T(8,128)S(1)}, u32[]{:S(2)}) copy-start(f32[64,5,16,512]{3,2,1,0:T(8,128)S(1)} %get-tuple-element.27) | copy-start | bytes 31457284
  49.4 30.5 %collective-permute-start.3 = (f32[64,1,5,8,128]{4,3,2,0,1:T(8,128)}, f32[64,1,5,8,128]{4,3,2,0,1:T(8,128)S(1)}, u32[]{:S(2)}, u32[]{:S(2)}) collective-permute-start(f32[64,1,5,8,128]{4,3,2,0,1:T(8,128)} %get-tuple-element.17), channel_id=1, source_target_pairs={{0,1},{1,0},{2,3},{3,2},{4,5},{5,4},{6,7},{7,6},{8,9},{9,8},{10,11... | collective-permute-start | bytes 3932168 | tf_op jit(solution)/shard_map/ppermute | solution.py:16
  50.9 7.0 %copy-start.1 = (f32[64,5,16]{2,1,0:T(8,128)S(1)}, f32[64,5,16]{2,1,0:T(8,128)}, u32[]{:S(2)}) copy-start(f32[64,5,16]{2,1,0:T(8,128)} %convert_reduce_fusion.1) | copy-start | bytes 61444
  50.9 28.2 %collective-permute-start.2 = (f32[64,1,5,8]{0,3,2,1:T(8,128)S(1)}, f32[64,1,5,8]{0,3,2,1:T(8,128)S(1)}, u32[]{:S(2)}, u32[]{:S(2)}) collective-permute-start(f32[64,1,5,8]{0,3,2,1:T(8,128)S(1)} %bitcast.107), channel_id=1, source_target_pairs={{0,1},{1,0},{2,3},{3,2},{4,5},{5,4},{6,7},{7,6},{8,9},{9,8},{10,11... | collective-permute-start | bytes 30728 | tf_op jit(solution)/shard_map/ppermute | solution.py:16
  58.3 21.2 %collective-permute-start.4 = (f32[64,1,5,8]{0,3,2,1:T(8,128)S(1)}, f32[64,1,5,8]{0,3,2,1:T(8,128)S(1)}, u32[]{:S(2)}, u32[]{:S(2)}) collective-permute-start(f32[64,1,5,8]{0,3,2,1:T(8,128)S(1)} %bitcast.108), channel_id=1, source_target_pairs={{0,1},{1,0},{2,3},{3,2},{4,5},{5,4},{6,7},{7,6},{8,9},{9,8},{10,11... | collective-permute-start | bytes 30728 | tf_op jit(solution)/shard_map/ppermute | solution.py:16
  82.2 67.2 %copy-start.4 = (bf16[1024,2048]{1,0:T(8,128)(2,1)S(1)}, bf16[1024,2048]{1,0:T(8,128)(2,1)}, u32[]{:S(2)}) copy-start(bf16[1024,2048]{1,0:T(8,128)(2,1)} %param.15) | copy-start | bytes 12582916
  162.5 0.7 copy-start.5
  162.5 5.9 %copy-start.2 = (bf16[320,128]{1,0:T(8,128)(2,1)S(1)}, bf16[320,128]{1,0:T(8,128)(2,1)}, u32[]{:S(2)}) copy-start(bf16[320,128]{1,0:T(8,128)(2,1)} %param.9) | copy-start | bytes 245764
  162.6 6.0 %copy-start.3 = (s32[64]{0:T(128)S(1)}, s32[64]{0:T(128)}, u32[]{:S(2)}) copy-start(s32[64]{0:T(128)} %param.13) | copy-start | bytes 772
  164.2 8.8 %all-to-all-start.1 = ((s32[8,1,8]{2,1,0:T(1,128)}), s32[8,1,8]{2,1,0:T(1,128)S(1)}, u32[]{:S(2)}, u32[]{:S(2)}) async-start(s32[8,1,8]{2,1,0:T(1,128)} %bitcast.26), calls=%async_computation.1 | async-start | bytes 8192 | tf_op jit(solution)/shard_map/all_to_all | solution.py:155
  173.0 8.9 %all-to-all-start.2 = ((bf16[8,8,640]{2,1,0:T(8,128)(2,1)}), bf16[8,8,640]{2,1,0:T(8,128)(2,1)S(1)}, u32[]{:S(2)}, u32[]{:S(2)}) async-start(bf16[8,8,640]{2,1,0:T(8,128)(2,1)} %fusion.11), calls=%async_computation.2 | async-start | bytes 163840 | tf_op jit(solution)/shard_map/all_to_all | solution.py:154
Sparse Core Ops, SparseCore 0:
  162.7 159.5 all-reduce.1
